TPU v7x, 32 devices: a whole 2x2x4 slice. The times are simulated.
32 devices in a mesh: rows: 16 (over z, x, core), feat: 2 (over y).
Axes of the slice: x: 2, y: 2, z: 4, core: 2. Of those that a mesh axis runs over, the one named last changes fastest.
Arguments:
- design: bfloat16 [16384, 16384], P('rows', 'feat'), may hold values from -6 to 6
- flags: int32 [16384], P('rows'), may hold values 0 or 1
- scales: float32 [16384], P('rows'), may hold values from 0.3 to 3
- damping: float32 [2, 8192], P('feat', 'rows'), may hold values from 0.2 to 2
- probes: float32 [32, 2, 8192], P(None, 'feat', 'rows'), may hold values from -6 to 6
Outputs:
- solution: float32 [32, 2, 8192], P(None, 'feat', 'rows')
- residual: float32 [32, 2, 8192], P(None, 'feat', 'rows')
All inputs are finite; a program needn't handle non-finite values. No bound on the sum of `flags` on one device may be relied on, other than what follows from the above.
Results may differ from a plain program's by a relative error of at most 0.0073.
Values may be sent and summed in bfloat16 or wider, within the bound.
A program may use at most 64 MiB of HBM per device.

v0:
```python
import jax
import jax.numpy as jnp
from jax import lax
from jax.sharding import PartitionSpec as P

ITERS = 2


def weigh(partial_value, wrow):
    summed = lax.psum(partial_value, "feat")
    return (wrow[None, :] * summed).astype(jnp.bfloat16)


def norms_block(resid):
    return lax.psum(jnp.sum(resid * resid, axis=1), "feat")


def shards(design, flags, scales, damping, probes):
    rows_dev = design.shape[0]
    total_rows = rows_dev * lax.axis_size("rows")
    wrow = flags.astype(jnp.float32) / (scales * scales) / total_rows
    columns = probes.shape[0]
    damp_full, rhs_full = (
        lax.all_gather(damping, "rows", axis=1, tiled=True),
        lax.all_gather(probes, "rows", axis=2, tiled=True),
    )
    damp = damp_full.reshape(-1)
    rhs = rhs_full.reshape(columns, -1)
    solution = jnp.zeros_like(rhs)
    residual = rhs
    direction = rhs
    norm_now = norms_block(residual)
    for step in range(ITERS):
        p_low = direction.astype(jnp.bfloat16)
        partial_value = lax.dot_general(
            p_low, design, (((1,), (1,)), ((), ())), preferred_element_type=jnp.float32
        )
        weighted = weigh(partial_value, wrow)
        term = jnp.dot(weighted, design, preferred_element_type=jnp.float32)
        image = lax.psum(term, "rows") + damp[None, :] * direction
        curve = lax.psum(jnp.sum(direction * image, axis=1), "feat")
        alpha = norm_now / curve
        solution = solution + alpha[:, None] * direction
        residual = residual - alpha[:, None] * image
        norm_next = norms_block(residual)
        direction = residual + (norm_next / norm_now)[:, None] * direction
        norm_now = norm_next
    width = probes.shape[2]
    offset = lax.axis_index("rows") * width
    own_solution = lax.dynamic_slice_in_dim(solution, offset, width, 1)
    own_residual = lax.dynamic_slice_in_dim(residual, offset, width, 1)
    return (own_solution.reshape(probes.shape), own_residual.reshape(probes.shape))


def solution(mesh):
    placed = (P("rows", "feat"), P("rows"), P("rows"), P("feat", "rows"), P(None, "feat", "rows"))
    return jax.shard_map(
        shards,
        mesh=mesh,
        in_specs=placed,
        out_specs=(P(None, "feat", "rows"), P(None, "feat", "rows")),
        check_vma=False,
    )
```

profile of v0, /device:TPU:0, one launch (start us, length us, event | category | flops | bytes accessed | tf_op | source)
XLA Modules:
  0.0 353.4 jit_solution(5223691146667350313)
XLA Ops:
  7.2 0.0 copy-start.2
  7.2 0.0 copy-start.1
  7.2 0.0 all-gather.2.cloned.1.call-start
  7.2 1.5 copy.7
  8.7 0.0 all-gather.2.cloned.1.call-update
  8.7 0.0 copy-start.3
  8.7 0.0 all-reduce.6.cloned.1.call-start
  8.8 42.6 %all-gather.2.cloned.1.call-done = f32[32,1,8192]{2,0,1:T(8,128)} async-done(((f32[32,1,512]{2,0,1:T(8,128)}), f32[32,1,8192]{2,0,1:T(8,128)}) %all-gather.2.cloned.1.call-update) | async-done | bytes 1048592 | tf_op jit(solution)/shard_map/all_gather | solution.py:25
  51.4 0.0 copy-start
  51.4 11.9 %fusion.11 = f32[32,1024]{1,0:T(8,128)} fusion(bf16[1024,8192]{1,0:T(8,128)(2,1)} %param.5, f32[32,1,8192]{2,0,1:T(8,128)} %all-gather.2.cloned.1.call-done), kind=kOutput, calls=%fused_computation.25 | convolution fusion | flops 536870912 | bytes 17956864 | tf_op jit(solution)/shard_map/dot_general | solution.py:35
  63.3 0.0 all-reduce.6.cloned.1.call-update
  63.3 0.0 all-reduce.8.cloned.1.call-start
  63.4 0.0 copy-done.2
  63.4 0.0 copy-done.1
  63.4 20.6 %all-reduce.6.cloned.1.call-done = f32[32,1024]{1,0:T(8,128)} async-done(((f32[32,1024]{1,0:T(8,128)}), f32[32,1024]{1,0:T(8,128)}) %all-reduce.6.cloned.1.call-update) | async-done | bytes 131088 | tf_op jit(solution)/shard_map/psum | solution.py:10
  84.0 9.8 %fusion.4 = f32[32,8192]{1,0:T(8,128)} fusion(bf16[1024,8192]{1,0:T(8,128)(2,1)} %param.5, f32[32,1024]{1,0:T(8,128)} %all-reduce.6.cloned.1.call-done, f32[1024]{0:T(1024)S(1)} %divide_multiply_fusion), kind=kOutput, calls=%fused_computation.14 | convolution fusion | flops 536936448 | bytes 17960960 | tf_op jit(solution)/shard_map/dot_general | solution.py:39
  93.8 0.0 all-reduce.8.cloned.1.call-update
  93.8 0.0 all-reduce.10.cloned.1.call-start
  93.9 0.0 copy-done.3
  93.9 21.7 %all_gather.7 = f32[1,8192]{1,0:T(1,128)S(1)} all-gather(f32[1,512]{1,0:T(1,128)S(1)} %copy-done.3), channel_id=1, replica_groups=mesh['rows'=16,'feat'=2] {'rows'}, dimensions={1}, use_global_device_ids=true | all-gather | bytes 34816 | tf_op jit(solution)/shard_map/all_gather | solution.py:24
  115.6 72.3 %all-reduce.8.cloned.1.call-done = f32[32,8192]{1,0:T(8,128)} async-done(((f32[32,8192]{1,0:T(8,128)}), f32[32,8192]{1,0:T(8,128)}) %all-reduce.8.cloned.1.call-update) | async-done | bytes 1048592 | tf_op jit(solution)/shard_map/psum | solution.py:40
  187.9 0.0 copy-done
  187.9 1.5 multiply_reduce_fusion.2
  189.5 4.9 %all-reduce = (f32[32]{0:T(128)S(1)}, f32[32]{0:T(128)S(1)}) all-reduce(f32[32]{0:T(128)S(1)} %get-tuple-element.3, f32[32]{0:T(128)S(1)} %get-tuple-element.2), channel_id=1, replica_groups=mesh['rows'=16,'feat'=2] {'feat'}, use_global_device_ids=true, to_apply=%region_1.0 | all-reduce | flops 64 | bytes 512 | tf_op jit(solution)/shard_map/psum | solution.py:15
  194.4 1.6 multiply_reduce_fusion.1
  196.0 4.9 %psum.60 = f32[32]{0:T(128)S(1)} all-reduce(f32[32]{0:T(128)S(1)} %get-tuple-element.8), channel_id=1, replica_groups=mesh['rows'=16,'feat'=2] {'feat'}, use_global_device_ids=true, to_apply=%region_7.0 | all-reduce | flops 32 | bytes 256 | tf_op jit(solution)/shard_map/psum | solution.py:15
  200.9 0.2 multiply_add_fusion.1
  201.1 11.5 %fusion = f32[32,1024]{1,0:T(8,128)} fusion(bf16[1024,8192]{1,0:T(8,128)(2,1)} %param.5, f32[32,8192]{1,0:T(8,128)S(1)} %multiply_add_fusion.1), kind=kOutput, calls=%fused_computation.8 | convolution fusion | flops 537133056 | bytes 17956864 | tf_op jit(solution)/shard_map/dot_general | solution.py:35
  212.6 0.0 all-reduce.10.cloned.1.call-update
  212.6 0.2 all-reduce.12.cloned.1.call-start
  212.8 20.6 %all-reduce.10.cloned.1.call-done = f32[32,1024]{1,0:T(8,128)} async-done(((f32[32,1024]{1,0:T(8,128)}), f32[32,1024]{1,0:T(8,128)}) %all-reduce.10.cloned.1.call-update) | async-done | bytes 131088 | tf_op jit(solution)/shard_map/psum | solution.py:10
  233.4 9.9 %fusion.5 = f32[32,8192]{1,0:T(8,128)} fusion(bf16[1024,8192]{1,0:T(8,128)(2,1)} %param.5, f32[32,1024]{1,0:T(8,128)} %all-reduce.10.cloned.1.call-done, f32[1024]{0:T(1024)S(1)} %divide_multiply_fusion), kind=kOutput, calls=%fused_computation.15 | convolution fusion | flops 536936448 | bytes 17960960 | tf_op jit(solution)/shard_map/dot_general | solution.py:39
  243.3 0.0 all-reduce.12.cloned.1.call-update
  243.3 93.8 %all-reduce.12.cloned.1.call-done = f32[32,8192]{1,0:T(8,128)} async-done(((f32[32,8192]{1,0:T(8,128)}), f32[32,8192]{1,0:T(8,128)}) %all-reduce.12.cloned.1.call-update) | async-done | bytes 1048592 | tf_op jit(solution)/shard_map/psum | solution.py:40
  337.1 2.5 multiply_reduce_fusion
  339.6 4.9 %psum.63 = f32[32]{0:T(128)S(1)} all-reduce(f32[32]{0:T(128)S(1)} %get-tuple-element.6), channel_id=1, replica_groups=mesh['rows'=16,'feat'=2] {'feat'}, use_global_device_ids=true, to_apply=%region_11.0 | all-reduce | flops 32 | bytes 256 | tf_op jit(solution)/shard_map/psum | solution.py:41
  344.6 0.9 dynamic-slice_subtract_fusion
  345.5 0.7 reshape.18
  346.2 0.7 reshape.19
  (4 shorter events, 0.0 us)
Async XLA Ops:
  7.2 56.2 %copy-start.2 = (s32[1024]{0:T(1024)S(1)}, s32[1024]{0:T(1024)}, u32[]{:S(2)}) copy-start(s32[1024]{0:T(1024)} %param.6) | copy-start | bytes 12292
  7.2 56.2 %copy-start.1 = (f32[1024]{0:T(1024)S(1)}, f32[1024]{0:T(1024)}, u32[]{:S(2)}) copy-start(f32[1024]{0:T(1024)} %param.7) | copy-start | bytes 12292
  7.2 44.2 %all-gather.2.cloned.1.call-start = ((), (), s32[]{:S(2)}) async-start(), calls=%async_computation | async-start | bytes 1114112 | tf_op jit(solution)/shard_map/all_gather | solution.py:25
  8.7 85.1 %copy-start.3 = (f32[1,512]{1,0:T(1,128)S(1)}, f32[1,512]{1,0:T(1,128)}, u32[]{:S(2)}) copy-start(f32[1,512]{1,0:T(1,128)} %param.8) | copy-start | bytes 6148
  8.7 75.2 %all-reduce.6.cloned.1.call-start = ((), (), s32[]{:S(2)}) async-start(), calls=%async_computation.1 | async-start | bytes 262144 | tf_op jit(solution)/shard_map/psum | solution.py:10
  51.4 136.5 %copy-start = (f32[32,1,8192]{2,0,1:T(8,128)S(1)}, f32[32,1,8192]{2,0,1:T(8,128)}, u32[]{:S(2)}) copy-start(f32[32,1,8192]{2,0,1:T(8,128)} %all-gather.2.cloned.1.call-done) | copy-start | bytes 3145732
  63.3 124.6 %all-reduce.8.cloned.1.call-start = ((), (), s32[]{:S(2)}) async-start(), calls=%async_computation.2 | async-start | bytes 2097152 | tf_op jit(solution)/shard_map/psum | solution.py:40
  93.8 139.6 %all-reduce.10.cloned.1.call-start = ((), (), s32[]{:S(2)}) async-start(), calls=%async_computation.3 | async-start | bytes 262144 | tf_op jit(solution)/shard_map/psum | solution.py:10
  212.6 124.5 %all-reduce.12.cloned.1.call-start = ((), (), s32[]{:S(2)}) async-start(), calls=%async_computation.4 | async-start | bytes 2097152 | tf_op jit(solution)/shard_map/psum | solution.py:40
Sparse Core Ops, SparseCore 0:
  10.8 40.5 all-gather.1
  63.4 20.5 all-reduce.5
  93.9 93.9 all-reduce.7
  212.7 20.6 all-reduce.9
  243.4 93.6 all-reduce.11
where the time goes:
time: 354 us; the launch traced here: 353 us
  waiting for transfers between devices  250 us (71%)
  matrix products  43 us (12%)
  blocking collectives  36.5 us (10%)
  between operations  13.9 us (4%)
  other arithmetic  6.75 us (2%)
    psum x2, waiting for transfers between devices, shards(): image = lax.psum(term, 'rows') + damp[None, :] * direction  166 us
    all_gather x1, waiting for transfers between devices, shards(): lax.all_gather(probes, 'rows', axis=2, tiled=True)  42.6 us
    psum x2, waiting for transfers between devices, weigh(): summed = lax.psum(partial_value, 'feat')  41.2 us
    dot_general x2, matrix products, shards(): lax.dot_general(p_low, design, (((1,), (1,)), ((), ())), preferred_elemen...  23.4 us
    all_gather x1, blocking collectives, shards(): lax.all_gather(damping, 'rows', axis=1, tiled=True)  21.7 us
    dot_general x2, matrix products, shards(): term = jnp.dot(weighted, design, preferred_element_type=jnp.float32)  19.7 us
    psum x2, blocking collectives, norms_block(): return lax.psum(jnp.sum(resid * resid, axis=1), 'feat')  9.86 us
  transfers between devices with their start and end apart: 5, of which 5 were waited for; matrix products, arithmetic and copies ran while one was open for 0% of the time, Pallas kernels for 0%

commit v1 on v0

--- a/solution.py
+++ b/solution.py
@@ -1,9 +1,16 @@
+import functools
+
 import jax
 import jax.numpy as jnp
 from jax import lax
+from jax.experimental import pallas as pl
+from jax.experimental.pallas import tpu as pltpu
 from jax.sharding import PartitionSpec as P
 
 ITERS = 2
+MESH = pl.DeviceIdType.MESH
+F32 = jnp.float32
+BF16 = jnp.bfloat16
 
 
 def weigh(partial_value, wrow):
@@ -52,10 +59,343 @@
     return (own_solution.reshape(probes.shape), own_residual.reshape(probes.shape))
 
 
+def solve_kernel(
+    depth, a_hbm, w_ref, d_ref, b_ref, x_ref, r_ref,
+    a, g, st, y, yr, yold, ss, ssr, ds, dr, xs, xr, zs, zr, tt, cs, cx, cz, p_ref,
+    a_sem, gs, gr, ss_s, ss_r, fs, fr, d_s, d_r, x_s, x_r, z_s, z_r, c_s, c_r,
+):
+    n = depth * 4
+    cols, width = b_ref.shape
+    me = lax.axis_index("rows")
+    feat = lax.axis_index("feat")
+    core = lax.rem(me, 2)
+    xx = lax.rem(me // 2, 2)
+    zz = me // 4
+
+    def rows_of(slot):
+        dz, dx, dc = slot // 4, (slot // 2) % 2, slot % 2
+        z1 = lax.rem(zz + dz, depth)
+        x1 = 1 - xx if dx else xx
+        c1 = 1 - core if dc else core
+        return (z1 * 2 + x1) * 2 + c1
+
+    def dev(slot):
+        return (rows_of(slot), feat)
+
+    other_feat = (me, 1 - feat)
+
+    far = list(range(1, depth))
+    order = [0, 1, 2] + [4 * k for k in far] + [3]
+    for e in (1, 2, 3):
+        order += [4 * k + e for k in far]
+
+    def load(slot):
+        start = pl.multiple_of(rows_of(slot) * width, width)
+        return pltpu.make_async_copy(
+            a_hbm.at[:, pl.ds(start, width)], a.at[slot], a_sem.at[slot]
+        )
+
+    for slot in order:
+        load(slot).start()
+
+    peers = [dev(1), dev(2)] + [dev(4 * k) for k in far] + [other_feat]
+    barrier = pltpu.get_barrier_semaphore()
+    for peer in peers:
+        pl.semaphore_signal(barrier, inc=1, device_id=peer, device_id_type=MESH)
+    pl.semaphore_wait(barrier, len(peers))
+
+    mask = lax.broadcasted_iota(jnp.int32, (cols, 128), 0) == lax.broadcasted_iota(
+        jnp.int32, (cols, 128), 1
+    )
+
+    def to_row(v):
+        return jnp.sum(jnp.where(mask, v, 0.0), axis=0, keepdims=True)
+
+    def to_col(t):
+        return jnp.sum(jnp.where(mask, t, 0.0), axis=1, keepdims=True)
+
+    def remote(src, dst, send, recv, target):
+        return pltpu.make_async_remote_copy(
+            src_ref=src, dst_ref=dst, send_sem=send, recv_sem=recv,
+            device_id=target, device_id_type=MESH,
+        )
+
+    x_ref[...] = jnp.zeros((cols, width), F32)
+    p_ref[...] = jnp.zeros((cols, width), F32)
+    r_ref[...] = b_ref[...]
+    yold[...] = jnp.zeros_like(yold)
+
+    def iteration(it, carry):
+        rr_old, dpp_old = carry
+        sent = []
+
+        def share(src_slot, dst_slot, target):
+            block = remote(
+                g.at[it, src_slot], g.at[it, dst_slot],
+                gs.at[it, dst_slot], gr.at[it, dst_slot], dev(target),
+            )
+            sums = remote(
+                st.at[it, src_slot], st.at[it, dst_slot],
+                ss_s.at[it, dst_slot], ss_r.at[it, dst_slot], dev(target),
+            )
+            block.start()
+            sums.start()
+            sent.extend([block, sums])
+
+        def arrive(slot):
+            remote(
+                g.at[it, slot], g.at[it, slot], gs.at[it, slot], gr.at[it, slot], dev(1)
+            ).wait_recv()
+            remote(
+                st.at[it, slot], st.at[it, slot],
+                ss_s.at[it, slot], ss_r.at[it, slot], dev(1),
+            ).wait_recv()
+
+        r = r_ref[...]
+        p = p_ref[...]
+        damp = d_ref[...]
+        g[it, 0] = r.astype(BF16)
+        dr_ = damp * r
+        st[it, 0] = jnp.zeros((8, 128), F32)
+        st[it, 0, 0:1] = to_row(jnp.sum(r * r, axis=1, keepdims=True))
+        st[it, 0, 1:2] = to_row(jnp.sum(dr_ * r, axis=1, keepdims=True))
+        st[it, 0, 2:3] = to_row(jnp.sum(dr_ * p, axis=1, keepdims=True))
+
+        for k in far:
+            share(0, 4 * (depth - k), 4 * k)
+        share(0, 2, 2)
+        share(0, 1, 1)
+
+        def product(slot, first=False):
+            @pl.when(it == 0)
+            def _():
+                load(slot).wait()
+
+            part = lax.dot_general(
+                g[it, slot], a[slot], (((1,), (1,)), ((), ())),
+                preferred_element_type=F32,
+            )
+            if first:
+                y[...] = part
+            else:
+                y[...] += part
+
+        product(0, True)
+        arrive(1)
+        product(1)
+        arrive(2)
+        share(2, 3, 1)
+        for k in far:
+            arrive(4 * k)
+            share(4 * k, 4 * k + 2, 2)
+            share(4 * k, 4 * k + 1, 1)
+        product(2)
+        for k in far:
+            product(4 * k)
+        arrive(3)
+        product(3)
+        for k in far:
+            arrive(4 * k + 2)
+            share(4 * k + 2, 4 * k + 3, 1)
+        for k in far:
+            arrive(4 * k + 1)
+            product(4 * k + 1)
+        for k in far:
+            product(4 * k + 2)
+        for k in far:
+            arrive(4 * k + 3)
+            product(4 * k + 3)
+
+        yc = remote(y, yr.at[it], fs.at[it, 0], fr.at[it, 0], other_feat)
+        yc.start()
+        total = st[it, 0]
+        for slot in range(1, n):
+            total = total + st[it, slot]
+        ss[it] = total
+        sc = remote(ss.at[it], ssr.at[it], fs.at[it, 1], fr.at[it, 1], other_feat)
+        sc.start()
+        sc.wait_recv()
+        sums = total + ssr[it]
+        rr = to_col(sums[0:1])
+        drr = to_col(sums[1:2])
+        drp = to_col(sums[2:3])
+        beta = jnp.where(it == 0, 0.0, rr / rr_old)
+        dpp = drr + 2.0 * beta * drp + beta * beta * dpp_old
+        p = r + beta * p
+        p_ref[...] = p
+        yc.wait_recv()
+        yy = y[...] + yr[it] + beta * yold[...]
+        yold[...] = yy
+        wy = w_ref[...] * yy
+        u = wy.astype(BF16)
+        curve_own = to_row(jnp.sum(wy * yy, axis=1, keepdims=True))
+        cs[it, 0] = jnp.broadcast_to(curve_own, (8, 128))
+
+        def small(src, dst, k, target):
+            copy = remote(src, dst, c_s.at[it, k], c_r.at[it, k], dev(target))
+            copy.start()
+            sent.append(copy)
+            return copy
+
+        c_die = small(cs.at[it, 0], cs.at[it, 1], 0, 1)
+
+        def term(slot):
+            return jnp.dot(u, a[slot], preferred_element_type=F32)
+
+        def to_die(k, dx):
+            i = 2 * k + dx
+            ds[it, i] = term(4 * k + 2 * dx + 1)
+            copy = remote(ds.at[it, i], dr.at[it, i], d_s.at[it, i], d_r.at[it, i], dev(1))
+            copy.start()
+            sent.append(copy)
+
+        def from_die(k, dx):
+            i = 2 * k + dx
+            remote(
+                ds.at[it, i], dr.at[it, i], d_s.at[it, i], d_r.at[it, i], dev(1)
+            ).wait_recv()
+            return dr[it, i]
+
+        zorder = far + [0]
+        for k in zorder:
+            to_die(k, 1)
+        c_die.wait_recv()
+        c_pair = cs[it, 0] + cs[it, 1]
+        cx[it, 0] = c_pair
+        c_x = small(cx.at[it, 0], cx.at[it, 1], 1, 2)
+        for k in zorder:
+            part = term(4 * k + 2)
+            xs[it, k] = (part + from_die(k, 1)).astype(BF16)
+            copy = remote(xs.at[it, k], xr.at[it, k], x_s.at[it, k], x_r.at[it, k], dev(2))
+            copy.start()
+            sent.append(copy)
+        for k in zorder:
+            to_die(k, 0)
+        c_x.wait_recv()
+        c_chip = cx[it, 0] + cx[it, 1]
+        cz[it, 0] = c_chip
+        c_z = [small(cz.at[it, 0], cz.at[it, depth - k], 1 + k, 4 * k) for k in far]
+        for k in zorder:
+            tt[k] = term(4 * k)
+
+        def chip_sum(k):
+            part = tt[k] + from_die(k, 0)
+            remote(
+                xs.at[it, k], xr.at[it, k], x_s.at[it, k], x_r.at[it, k], dev(2)
+            ).wait_recv()
+            return part + xr[it, k].astype(F32)
+
+        for k in far:
+            zs[it, k] = chip_sum(k).astype(BF16)
+            copy = remote(
+                zs.at[it, k], zr.at[it, depth - k],
+                z_s.at[it, k], z_r.at[it, depth - k], dev(4 * k),
+            )
+            copy.start()
+            sent.append(copy)
+        image = chip_sum(0) + damp * p
+        curve_row = cz[it, 0]
+        for k in far:
+            remote(
+                cz.at[it, 0], cz.at[it, k], c_s.at[it, 1 + k], c_r.at[it, 1 + depth - k],
+                dev(4 * k),
+            ).wait_recv()
+            curve_row = curve_row + cz[it, k]
+        alpha = rr / (to_col(curve_row[0:1]) + dpp)
+        x_ref[...] += alpha * p
+        for k in far:
+            remote(
+                zs.at[it, k], zr.at[it, k], z_s.at[it, k], z_r.at[it, k], dev(4 * k)
+            ).wait_recv()
+            image = image + zr[it, k].astype(F32)
+        r_ref[...] = r - alpha * image
+
+        yc.wait_send()
+        sc.wait_send()
+        for copy in sent:
+            copy.wait_send()
+        return rr, dpp
+
+    ones = jnp.ones((cols, 1), F32)
+    lax.fori_loop(0, ITERS, iteration, (ones, jnp.zeros((cols, 1), F32)))
+
+
+def fused(depth, design, flags, scales, damping, probes):
+    rows_dev = design.shape[0]
+    n = depth * 4
+    total_rows = rows_dev * n
+    wrow = flags.astype(F32) / (scales * scales) / total_rows
+    cols, _, width = probes.shape
+    vm = pl.BlockSpec(memory_space=pltpu.VMEM)
+    v = pltpu.VMEM
+    dma = pltpu.SemaphoreType.DMA
+    out = jax.ShapeDtypeStruct((cols, width), F32)
+    i2 = ITERS
+    x, r = pl.pallas_call(
+        functools.partial(solve_kernel, depth),
+        out_shape=(out, out),
+        in_specs=[pl.BlockSpec(memory_space=pl.ANY), vm, vm, vm],
+        out_specs=(vm, vm),
+        scratch_shapes=[
+            v((n, rows_dev, width), BF16),
+            v((i2, n, cols, width), BF16),
+            v((i2, n, 8, 128), F32),
+            v((cols, rows_dev), F32),
+            v((i2, cols, rows_dev), F32),
+            v((cols, rows_dev), F32),
+            v((i2, 8, 128), F32),
+            v((i2, 8, 128), F32),
+            v((i2, 2 * depth, cols, width), F32),
+            v((i2, 2 * depth, cols, width), F32),
+            v((i2, depth, cols, width), BF16),
+            v((i2, depth, cols, width), BF16),
+            v((i2, depth, cols, width), BF16),
+            v((i2, depth, cols, width), BF16),
+            v((depth, cols, width), F32),
+            v((i2, 2, 8, 128), F32),
+            v((i2, 2, 8, 128), F32),
+            v((i2, depth, 8, 128), F32),
+            v((cols, width), F32),
+            dma((n,)),
+            dma((i2, n)),
+            dma((i2, n)),
+            dma((i2, n)),
+            dma((i2, n)),
+            dma((i2, 2)),
+            dma((i2, 2)),
+            dma((i2, 2 * depth)),
+            dma((i2, 2 * depth)),
+            dma((i2, depth)),
+            dma((i2, depth)),
+            dma((i2, depth)),
+            dma((i2, depth)),
+            dma((i2, depth + 1)),
+            dma((i2, depth + 1)),
+        ],
+        compiler_params=pltpu.CompilerParams(
+            collective_id=0, has_side_effects=True, vmem_limit_bytes=48 * 1024 * 1024
+        ),
+    )(design, wrow.reshape(1, rows_dev), damping, probes.reshape(cols, width))
+    return x.reshape(probes.shape), r.reshape(probes.shape)
+
+
 def solution(mesh):
     placed = (P("rows", "feat"), P("rows"), P("rows"), P("feat", "rows"), P(None, "feat", "rows"))
+    rows, feats = mesh.shape["rows"], mesh.shape["feat"]
+
+    def body(design, flags, scales, damping, probes):
+        fits = (
+            feats == 2 and rows % 4 == 0 and 8 <= rows <= 16
+            and probes.shape[2] % 256 == 0 and design.shape[0] % 256 == 0
+            and design.size <= 1 << 23 and probes.shape[0] % 16 == 0
+            and probes.shape[0] <= 32
+        )
+        if fits:
+            return fused(rows // 4, design, flags, scales, damping, probes)
+        return shards(design, flags, scales, damping, probes)
+
     return jax.shard_map(
-        shards,
+        body,
         mesh=mesh,
         in_specs=placed,
         out_specs=(P(None, "feat", "rows"), P(None, "feat", "rows")),

time: 354 us -> 62.1 us (0.18)
  waiting for transfers between devices: 250 us -> 0 us
  Pallas kernels: 0 us -> 57.6 us
  matrix products: 43 us -> 0 us
  blocking collectives: 36.5 us -> 0 us
  between operations: 13.9 us -> 0.64 us
  other arithmetic: 6.75 us -> 0.71 us
    psum x4 -> x0, waiting for transfers between devices: 207 us -> none  [the longest x2 166 us: shards(): image = lax.psum(term, 'rows') + damp[None, :] * direction]
    pallas_call x0 -> x1, Pallas kernels: none -> 57.6 us  [fused(): pl.pallas_call(functools.partial(solve_kernel, depth), out_shape=(out, ou...]
    dot_general x4 -> x0, matrix products: 43 us -> none  [the longest x2 23.4 us: shards(): lax.dot_general(p_low, design, (((1,), (1,)), ((), ())), preferred_elemen...]
    all_gather x1 -> x0, waiting for transfers between devices: 42.6 us -> none  [shards(): lax.all_gather(probes, 'rows', axis=2, tiled=True)]
    all_gather x1 -> x0, blocking collectives: 21.7 us -> none  [shards(): lax.all_gather(damping, 'rows', axis=1, tiled=True)]
    psum x3 -> x0, blocking collectives: 14.8 us -> none  [the longest x2 9.86 us: norms_block(): return lax.psum(jnp.sum(resid * resid, axis=1), 'feat')]
    reduce_sum x3 -> x0, other arithmetic: 5.62 us -> none  [the longest x2 4.04 us: shards(): curve = lax.psum(jnp.sum(direction * image, axis=1), 'feat')]
  transfers between devices with their start and end apart: 5 -> 0, of which waited for: 5 -> 0; matrix products, arithmetic and copies ran while one was open for 0% -> 0% of each run, Pallas kernels for 0% -> 0%
where the time goes in v1:
time: 62.1 us; the launch traced here: 61.9 us
  Pallas kernels  57.6 us (93%)
  local copies, waits for them, and re-layouts  2.92 us (5%)
  other arithmetic  0.71 us (1%)
  between operations  0.64 us (1%)
    pallas_call x1, Pallas kernels, fused(): pl.pallas_call(functools.partial(solve_kernel, depth), out_shape=(out, ou...  57.6 us
    unnamed x5, local copies, waits for them, and re-layouts  2.92 us

profile of v1, /device:TPU:0, one launch (start us, length us, event | category | flops | bytes accessed | tf_op | source)
XLA Modules:
  0.0 61.9 jit_solution(12353726193177133468)
XLA Ops:
  0.6 0.7 %divide_multiply_fusion = f32[1024]{0:T(1024)S(1)} fusion(f32[1024]{0:T(1024)} %param.7, s32[1024]{0:T(1024)} %param.6), kind=kLoop, calls=%fused_computation.1 | loop fusion | flops 4096 | bytes 12288 | tf_op jit(solution)/shard_map/div | solution.py:327
  1.3 0.8 %copy.11 = f32[32,1,512]{2,0,1:T(8,128)S(1)} copy(f32[32,1,512]{2,1,0:T(1,128)} %param.9) | data formatting | bytes 131072
  2.2 0.0 copy-start
  2.2 0.7 %copy-done = f32[1,512]{1,0:T(1,128)S(1)} copy-done((f32[1,512]{1,0:T(1,128)S(1)}, f32[1,512]{1,0:T(1,128)}, u32[]{:S(2)}) %copy-start) | copy-done | bytes 2072
  2.9 57.6 %shard_map.68 = (f32[32,512]{1,0:T(8,128)S(1)}, f32[32,512]{1,0:T(8,128)S(1)}) custom-call(bf16[1024,8192]{1,0:T(8,128)(2,1)} %a_hbm.1, f32[1,1024]{1,0:T(1,128)S(1)} %bitcast.9, f32[1,512]{1,0:T(1,128)S(1)} %copy-done, f32[32,512]{1,0:T(8,128)S(1)} %bitcast.6), custom_call_target="tpu_custom_call" | custom-call | tf_op jit(solution)/shard_map/pallas_call | solution.py:334
  60.5 0.7 %copy.7 = f32[32,1,512]{2,1,0:T(1,128)} copy(f32[32,1,512]{2,0,1:T(8,128)S(1)} %bitcast.8) | data formatting | bytes 131072
  61.2 0.7 %copy.8 = f32[32,1,512]{2,1,0:T(1,128)} copy(f32[32,1,512]{2,0,1:T(8,128)S(1)} %bitcast.7) | data formatting | bytes 131072
Async XLA Ops:
  2.2 0.7 %copy-start = (f32[1,512]{1,0:T(1,128)S(1)}, f32[1,512]{1,0:T(1,128)}, u32[]{:S(2)}) copy-start(f32[1,512]{1,0:T(1,128)} %d_ref.1) | copy-start | bytes 6148

commit v2 on v1

--- a/solution.py
+++ b/solution.py
@@ -60,45 +60,62 @@
 
 
 def solve_kernel(
-    depth, a_hbm, w_ref, d_ref, b_ref, x_ref, r_ref,
-    a, g, st, y, yr, yold, ss, ssr, ds, dr, xs, xr, zs, zr, tt, cs, cx, cz, p_ref,
-    a_sem, gs, gr, ss_s, ss_r, fs, fr, d_s, d_r, x_s, x_r, z_s, z_r, c_s, c_r,
+    depth, total_rows, a_hbm, flags_in, scales_in, d_in, b_in, x_ref, r_ref,
+    flags_ref, scales_ref, d_ref, b_ref, w_ref,
+    a, g, st, y, yr, yold, ss, ssr, ds, dr, xs, xr, zs, zr, tt, cs, p_ref,
+    in_sem, a_sem, gs, gr, ss_s, ss_r, fs, fr, d_s, d_r, x_s, x_r, z_s, z_r, c_s, c_r,
 ):
     n = depth * 4
-    cols, width = b_ref.shape
+    cols, width = x_ref.shape
     me = lax.axis_index("rows")
     feat = lax.axis_index("feat")
     core = lax.rem(me, 2)
     xx = lax.rem(me // 2, 2)
     zz = me // 4
 
-    def rows_of(slot):
-        dz, dx, dc = slot // 4, (slot // 2) % 2, slot % 2
+    def rows_of(dz, dx, dc):
         z1 = lax.rem(zz + dz, depth)
         x1 = 1 - xx if dx else xx
         c1 = 1 - core if dc else core
         return (z1 * 2 + x1) * 2 + c1
 
-    def dev(slot):
-        return (rows_of(slot), feat)
+    def dev(dz, dx, dc):
+        return (rows_of(dz, dx, dc), feat)
+
+    die, side = dev(0, 0, 1), dev(0, 1, 0)
 
     other_feat = (me, 1 - feat)
 
+    upper = (zz * 2) // depth
     far = list(range(1, depth))
-    order = [0, 1, 2] + [4 * k for k in far] + [3]
-    for e in (1, 2, 3):
-        order += [4 * k + e for k in far]
-
-    def load(slot):
-        start = pl.multiple_of(rows_of(slot) * width, width)
+    away = [k * upper + (depth - k) * (1 - upper) for k in far]
+    near = [depth - k for k in away]
+
+    def load(dz, e):
+        start = pl.multiple_of(rows_of(dz, e // 2, e % 2) * width, width)
+        slot = dz * 4 + e
         return pltpu.make_async_copy(
             a_hbm.at[:, pl.ds(start, width)], a.at[slot], a_sem.at[slot]
         )
 
-    for slot in order:
-        load(slot).start()
-
-    peers = [dev(1), dev(2)] + [dev(4 * k) for k in far] + [other_feat]
+    small_loads = [
+        pltpu.make_async_copy(src, dst, in_sem.at[i])
+        for i, (src, dst) in enumerate(
+            [(b_in, b_ref), (d_in, d_ref), (flags_in, flags_ref), (scales_in, scales_ref)]
+        )
+    ]
+    for copy in small_loads:
+        copy.start()
+    for e in range(3):
+        load(0, e).start()
+    for k in near:
+        load(k, 0).start()
+    load(0, 3).start()
+    for e in range(1, 4):
+        for k in near:
+            load(k, e).start()
+
+    peers = [die, side] + [dev(k, 0, 0) for k in far] + [other_feat]
     barrier = pltpu.get_barrier_semaphore()
     for peer in peers:
         pl.semaphore_signal(barrier, inc=1, device_id=peer, device_id_type=MESH)
@@ -122,7 +139,11 @@
 
     x_ref[...] = jnp.zeros((cols, width), F32)
     p_ref[...] = jnp.zeros((cols, width), F32)
-    r_ref[...] = b_ref[...]
+    for copy in small_loads:
+        copy.wait()
+    r_ref[...] = b_ref[:, 0, :]
+    scale = scales_ref[...]
+    w_ref[...] = flags_ref[...].astype(F32) / (scale * scale) / total_rows
     yold[...] = jnp.zeros_like(yold)
 
     def iteration(it, carry):
@@ -132,44 +153,71 @@
         def share(src_slot, dst_slot, target):
             block = remote(
                 g.at[it, src_slot], g.at[it, dst_slot],
-                gs.at[it, dst_slot], gr.at[it, dst_slot], dev(target),
-            )
-            sums = remote(
-                st.at[it, src_slot], st.at[it, dst_slot],
-                ss_s.at[it, dst_slot], ss_r.at[it, dst_slot], dev(target),
+                gs.at[it, dst_slot], gr.at[it, dst_slot], target,
             )
             block.start()
-            sums.start()
-            sent.extend([block, sums])
+            sent.append(block)
 
         def arrive(slot):
             remote(
-                g.at[it, slot], g.at[it, slot], gs.at[it, slot], gr.at[it, slot], dev(1)
+                g.at[it, slot], g.at[it, slot], gs.at[it, slot], gr.at[it, slot], die
             ).wait_recv()
+
+        def tell(buf, send, recv, src, dst, k, target):
+            copy = remote(
+                buf.at[it, src], buf.at[it, dst], send.at[it, k], recv.at[it, k], target
+            )
+            copy.start()
+            sent.append(copy)
+
+        def hear(buf, send, recv, dst, k):
             remote(
-                st.at[it, slot], st.at[it, slot],
-                ss_s.at[it, slot], ss_r.at[it, slot], dev(1),
+                buf.at[it, dst], buf.at[it, dst], send.at[it, k], recv.at[it, k], die
             ).wait_recv()
 
         r = r_ref[...]
         p = p_ref[...]
         damp = d_ref[...]
         g[it, 0] = r.astype(BF16)
+        for k in away:
+            share(0, 4 * (depth - k), dev(k, 0, 0))
+        share(0, 2, side)
+        share(0, 1, die)
+
+        def reduce_start(buf, send, recv):
+            tell(buf, send, recv, 0, 1, 0, die)
+
+        def reduce_x(buf, send, recv):
+            hear(buf, send, recv, 1, 0)
+            buf[it, 2] = buf[it, 0] + buf[it, 1]
+            tell(buf, send, recv, 2, 3, 1, side)
+
+        def reduce_z(buf, send, recv):
+            hear(buf, send, recv, 3, 1)
+            buf[it, 4] = buf[it, 2] + buf[it, 3]
+            for k in far:
+                tell(buf, send, recv, 4, 4 + depth - k, 1 + depth - k, dev(k, 0, 0))
+
+        def reduce_end(buf, send, recv):
+            total = buf[it, 4]
+            for k in far:
+                hear(buf, send, recv, 4 + k, 1 + k)
+                total = total + buf[it, 4 + k]
+            return total
+
         dr_ = damp * r
         st[it, 0] = jnp.zeros((8, 128), F32)
         st[it, 0, 0:1] = to_row(jnp.sum(r * r, axis=1, keepdims=True))
         st[it, 0, 1:2] = to_row(jnp.sum(dr_ * r, axis=1, keepdims=True))
         st[it, 0, 2:3] = to_row(jnp.sum(dr_ * p, axis=1, keepdims=True))
-
-        for k in far:
-            share(0, 4 * (depth - k), 4 * k)
-        share(0, 2, 2)
-        share(0, 1, 1)
-
-        def product(slot, first=False):
+        reduce_start(st, ss_s, ss_r)
+
+        def product(dz, e, first=False):
+            slot = dz * 4 + e
+
             @pl.when(it == 0)
             def _():
-                load(slot).wait()
+                load(dz, e).wait()
 
             part = lax.dot_general(
                 g[it, slot], a[slot], (((1,), (1,)), ((), ())),
@@ -180,37 +228,37 @@
             else:
                 y[...] += part
 
-        product(0, True)
+        product(0, 0, True)
+        reduce_x(st, ss_s, ss_r)
         arrive(1)
-        product(1)
+        product(0, 1)
         arrive(2)
-        share(2, 3, 1)
-        for k in far:
+        share(2, 3, die)
+        for k in near:
             arrive(4 * k)
-            share(4 * k, 4 * k + 2, 2)
-            share(4 * k, 4 * k + 1, 1)
-        product(2)
-        for k in far:
-            product(4 * k)
+            share(4 * k, 4 * k + 2, side)
+            share(4 * k, 4 * k + 1, die)
+        reduce_z(st, ss_s, ss_r)
+        product(0, 2)
+        for k in near:
+            product(k, 0)
         arrive(3)
-        product(3)
-        for k in far:
+        product(0, 3)
+        for k in near:
             arrive(4 * k + 2)
-            share(4 * k + 2, 4 * k + 3, 1)
-        for k in far:
+            share(4 * k + 2, 4 * k + 3, die)
+        for k in near:
             arrive(4 * k + 1)
-            product(4 * k + 1)
-        for k in far:
-            product(4 * k + 2)
-        for k in far:
+            product(k, 1)
+        for k in near:
+            product(k, 2)
+        for k in near:
             arrive(4 * k + 3)
-            product(4 * k + 3)
+            product(k, 3)
 
         yc = remote(y, yr.at[it], fs.at[it, 0], fr.at[it, 0], other_feat)
         yc.start()
-        total = st[it, 0]
-        for slot in range(1, n):
-            total = total + st[it, slot]
+        total = reduce_end(st, ss_s, ss_r)
         ss[it] = total
         sc = remote(ss.at[it], ssr.at[it], fs.at[it, 1], fr.at[it, 1], other_feat)
         sc.start()
@@ -231,13 +279,7 @@
         curve_own = to_row(jnp.sum(wy * yy, axis=1, keepdims=True))
         cs[it, 0] = jnp.broadcast_to(curve_own, (8, 128))
 
-        def small(src, dst, k, target):
-            copy = remote(src, dst, c_s.at[it, k], c_r.at[it, k], dev(target))
-            copy.start()
-            sent.append(copy)
-            return copy
-
-        c_die = small(cs.at[it, 0], cs.at[it, 1], 0, 1)
+        reduce_start(cs, c_s, c_r)
 
         def term(slot):
             return jnp.dot(u, a[slot], preferred_element_type=F32)
@@ -245,67 +287,55 @@
         def to_die(k, dx):
             i = 2 * k + dx
             ds[it, i] = term(4 * k + 2 * dx + 1)
-            copy = remote(ds.at[it, i], dr.at[it, i], d_s.at[it, i], d_r.at[it, i], dev(1))
+            copy = remote(ds.at[it, i], dr.at[it, i], d_s.at[it, i], d_r.at[it, i], die)
             copy.start()
             sent.append(copy)
 
         def from_die(k, dx):
             i = 2 * k + dx
             remote(
-                ds.at[it, i], dr.at[it, i], d_s.at[it, i], d_r.at[it, i], dev(1)
+                ds.at[it, i], dr.at[it, i], d_s.at[it, i], d_r.at[it, i], die
             ).wait_recv()
             return dr[it, i]
 
-        zorder = far + [0]
+        zorder = away + [0]
         for k in zorder:
             to_die(k, 1)
-        c_die.wait_recv()
-        c_pair = cs[it, 0] + cs[it, 1]
-        cx[it, 0] = c_pair
-        c_x = small(cx.at[it, 0], cx.at[it, 1], 1, 2)
+        reduce_x(cs, c_s, c_r)
         for k in zorder:
             part = term(4 * k + 2)
             xs[it, k] = (part + from_die(k, 1)).astype(BF16)
-            copy = remote(xs.at[it, k], xr.at[it, k], x_s.at[it, k], x_r.at[it, k], dev(2))
+            copy = remote(xs.at[it, k], xr.at[it, k], x_s.at[it, k], x_r.at[it, k], side)
             copy.start()
             sent.append(copy)
         for k in zorder:
             to_die(k, 0)
-        c_x.wait_recv()
-        c_chip = cx[it, 0] + cx[it, 1]
-        cz[it, 0] = c_chip
-        c_z = [small(cz.at[it, 0], cz.at[it, depth - k], 1 + k, 4 * k) for k in far]
+        reduce_z(cs, c_s, c_r)
         for k in zorder:
             tt[k] = term(4 * k)
 
         def chip_sum(k):
             part = tt[k] + from_die(k, 0)
             remote(
-                xs.at[it, k], xr.at[it, k], x_s.at[it, k], x_r.at[it, k], dev(2)
+                xs.at[it, k], xr.at[it, k], x_s.at[it, k], x_r.at[it, k], side
             ).wait_recv()
             return part + xr[it, k].astype(F32)
 
-        for k in far:
+        for k in away:
             zs[it, k] = chip_sum(k).astype(BF16)
             copy = remote(
                 zs.at[it, k], zr.at[it, depth - k],
-                z_s.at[it, k], z_r.at[it, depth - k], dev(4 * k),
+                z_s.at[it, k], z_r.at[it, depth - k], dev(k, 0, 0),
             )
             copy.start()
             sent.append(copy)
         image = chip_sum(0) + damp * p
-        curve_row = cz[it, 0]
-        for k in far:
-            remote(
-                cz.at[it, 0], cz.at[it, k], c_s.at[it, 1 + k], c_r.at[it, 1 + depth - k],
-                dev(4 * k),
-            ).wait_recv()
-            curve_row = curve_row + cz[it, k]
+        curve_row = reduce_end(cs, c_s, c_r)
         alpha = rr / (to_col(curve_row[0:1]) + dpp)
         x_ref[...] += alpha * p
         for k in far:
             remote(
-                zs.at[it, k], zr.at[it, k], z_s.at[it, k], z_r.at[it, k], dev(4 * k)
+                zs.at[it, k], zr.at[it, k], z_s.at[it, k], z_r.at[it, k], die
             ).wait_recv()
             image = image + zr[it, k].astype(F32)
         r_ref[...] = r - alpha * image
@@ -324,7 +354,6 @@
     rows_dev = design.shape[0]
     n = depth * 4
     total_rows = rows_dev * n
-    wrow = flags.astype(F32) / (scales * scales) / total_rows
     cols, _, width = probes.shape
     vm = pl.BlockSpec(memory_space=pltpu.VMEM)
     v = pltpu.VMEM
@@ -332,14 +361,19 @@
     out = jax.ShapeDtypeStruct((cols, width), F32)
     i2 = ITERS
     x, r = pl.pallas_call(
-        functools.partial(solve_kernel, depth),
+        functools.partial(solve_kernel, depth, total_rows),
         out_shape=(out, out),
-        in_specs=[pl.BlockSpec(memory_space=pl.ANY), vm, vm, vm],
+        in_specs=[pl.BlockSpec(memory_space=pl.ANY)] * 5,
         out_specs=(vm, vm),
         scratch_shapes=[
+            v((1, rows_dev), jnp.int32),
+            v((1, rows_dev), F32),
+            v((1, width), F32),
+            v((cols, 1, width), F32),
+            v((1, rows_dev), F32),
             v((n, rows_dev, width), BF16),
             v((i2, n, cols, width), BF16),
-            v((i2, n, 8, 128), F32),
+            v((i2, depth + 4, 8, 128), F32),
             v((cols, rows_dev), F32),
             v((i2, cols, rows_dev), F32),
             v((cols, rows_dev), F32),
@@ -352,15 +386,14 @@
             v((i2, depth, cols, width), BF16),
             v((i2, depth, cols, width), BF16),
             v((depth, cols, width), F32),
-            v((i2, 2, 8, 128), F32),
-            v((i2, 2, 8, 128), F32),
-            v((i2, depth, 8, 128), F32),
+            v((i2, depth + 4, 8, 128), F32),
             v((cols, width), F32),
+            dma((4,)),
             dma((n,)),
             dma((i2, n)),
             dma((i2, n)),
-            dma((i2, n)),
-            dma((i2, n)),
+            dma((i2, depth + 1)),
+            dma((i2, depth + 1)),
             dma((i2, 2)),
             dma((i2, 2)),
             dma((i2, 2 * depth)),
@@ -375,7 +408,7 @@
         compiler_params=pltpu.CompilerParams(
             collective_id=0, has_side_effects=True, vmem_limit_bytes=48 * 1024 * 1024
         ),
-    )(design, wrow.reshape(1, rows_dev), damping, probes.reshape(cols, width))
+    )(design, flags.reshape(1, rows_dev), scales.reshape(1, rows_dev), damping, probes)
     return x.reshape(probes.shape), r.reshape(probes.shape)
 
 

time: 62.1 us -> 61.7 us (level)
  local copies, waits for them, and re-layouts: 2.92 us -> 4.28 us
  Pallas kernels: 57.6 us -> 56.5 us
  other arithmetic: 0.71 us -> 0 us
    unnamed x5 -> x10, local copies, waits for them, and re-layouts: 2.92 us -> 4.28 us
    pallas_call x1, Pallas kernels: 57.6 us -> 56.5 us  [fused(): pl.pallas_call(functools.partial(solve_kernel, depth, total_rows), out_sh...]
    div x1 -> x0, other arithmetic: 0.71 us -> none  [fused(): wrow = flags.astype(F32) / (scales * scales) / total_rows]
where the time goes in v2:
time: 61.7 us; the launch traced here: 61.4 us
  Pallas kernels  56.5 us (92%)
  local copies, waits for them, and re-layouts  4.28 us (7%)
  between operations  0.65 us (1%)
    pallas_call x1, Pallas kernels, fused(): pl.pallas_call(functools.partial(solve_kernel, depth, total_rows), out_sh...  56.5 us
    unnamed x10, local copies, waits for them, and re-layouts  4.28 us

profile of v2, /device:TPU:0, one launch (start us, length us, event | category | flops | bytes accessed | tf_op | source)
XLA Modules:
  0.0 61.4 jit_solution(10859916043407683157)
XLA Ops:
  0.6 0.0 copy-start
  0.6 0.8 %copy-done = f32[32,1,512]{2,1,0:T(1,128)S(1)} copy-done((f32[32,1,512]{2,1,0:T(1,128)S(1)}, f32[32,1,512]{2,1,0:T(1,128)}, u32[]{:S(2)}) %copy-start) | copy-done | bytes 65560
  1.5 0.0 copy-start.1
  1.5 0.7 %copy-done.1 = s32[1024]{0:T(1024)S(1)} copy-done((s32[1024]{0:T(1024)S(1)}, s32[1024]{0:T(1024)}, u32[]{:S(2)}) %copy-start.1) | copy-done | bytes 4120
  2.2 0.0 copy-start.2
  2.2 0.7 %copy-done.2 = f32[1024]{0:T(1024)S(1)} copy-done((f32[1024]{0:T(1024)S(1)}, f32[1024]{0:T(1024)}, u32[]{:S(2)}) %copy-start.2) | copy-done | bytes 4120
  2.8 0.0 copy-start.3
  2.8 0.7 %copy-done.3 = f32[1,512]{1,0:T(1,128)S(1)} copy-done((f32[1,512]{1,0:T(1,128)S(1)}, f32[1,512]{1,0:T(1,128)}, u32[]{:S(2)}) %copy-start.3) | copy-done | bytes 2072
  3.5 56.5 %shard_map.68 = (f32[32,512]{1,0:T(8,128)S(1)}, f32[32,512]{1,0:T(8,128)S(1)}) custom-call(bf16[1024,8192]{1,0:T(8,128)(2,1)} %a_hbm.1, s32[1,1024]{1,0:T(1,128)S(1)} %bitcast.6, f32[1,1024]{1,0:T(1,128)S(1)} %bitcast.7, f32[1,512]{1,0:T(1,128)S(1)} %copy-done.3, f32[32,1,512]{2,1,0:T(1,128)S(1)} %copy-done), custom_call_target="tpu_custom_call" | custom-call | tf_op jit(solution)/shard_map/pallas_call | solution.py:363
  60.0 0.7 %copy.7 = f32[32,1,512]{2,1,0:T(1,128)} copy(f32[32,1,512]{2,0,1:T(8,128)S(1)} %bitcast.5) | data formatting | bytes 131072
  60.7 0.7 %copy.8 = f32[32,1,512]{2,1,0:T(1,128)} copy(f32[32,1,512]{2,0,1:T(8,128)S(1)} %bitcast.4) | data formatting | bytes 131072
Async XLA Ops:
  0.6 0.8 %copy-start = (f32[32,1,512]{2,1,0:T(1,128)S(1)}, f32[32,1,512]{2,1,0:T(1,128)}, u32[]{:S(2)}) copy-start(f32[32,1,512]{2,1,0:T(1,128)} %b_in.1) | copy-start | bytes 196612
  1.5 0.7 %copy-start.1 = (s32[1024]{0:T(1024)S(1)}, s32[1024]{0:T(1024)}, u32[]{:S(2)}) copy-start(s32[1024]{0:T(1024)} %param.6) | copy-start | bytes 12292
  2.2 0.7 %copy-start.2 = (f32[1024]{0:T(1024)S(1)}, f32[1024]{0:T(1024)}, u32[]{:S(2)}) copy-start(f32[1024]{0:T(1024)} %param.7) | copy-start | bytes 12292
  2.8 0.7 %copy-start.3 = (f32[1,512]{1,0:T(1,128)S(1)}, f32[1,512]{1,0:T(1,128)}, u32[]{:S(2)}) copy-start(f32[1,512]{1,0:T(1,128)} %d_in.1) | copy-start | bytes 6148

commit v3 on v2

--- a/solution.py
+++ b/solution.py
@@ -62,7 +62,7 @@
 def solve_kernel(
     depth, total_rows, a_hbm, flags_in, scales_in, d_in, b_in, x_ref, r_ref,
     flags_ref, scales_ref, d_ref, b_ref, w_ref,
-    a, g, st, y, yr, yold, ss, ssr, ds, dr, xs, xr, zs, zr, tt, cs, p_ref,
+    a, g, st, y, ylow, yr, yold, ss, ssr, ds, dr, xs, xr, zs, zr, tt, cs, p_ref,
     in_sem, a_sem, gs, gr, ss_s, ss_r, fs, fr, d_s, d_r, x_s, x_r, z_s, z_r, c_s, c_r,
 ):
     n = depth * 4
@@ -86,9 +86,8 @@
 
     other_feat = (me, 1 - feat)
 
-    upper = (zz * 2) // depth
     far = list(range(1, depth))
-    away = [k * upper + (depth - k) * (1 - upper) for k in far]
+    away = far
     near = [depth - k for k in away]
 
     def load(dz, e):
@@ -256,7 +255,8 @@
             arrive(4 * k + 3)
             product(k, 3)
 
-        yc = remote(y, yr.at[it], fs.at[it, 0], fr.at[it, 0], other_feat)
+        ylow[...] = y[...].astype(BF16)
+        yc = remote(ylow, yr.at[it], fs.at[it, 0], fr.at[it, 0], other_feat)
         yc.start()
         total = reduce_end(st, ss_s, ss_r)
         ss[it] = total
@@ -272,7 +272,7 @@
         p = r + beta * p
         p_ref[...] = p
         yc.wait_recv()
-        yy = y[...] + yr[it] + beta * yold[...]
+        yy = y[...] + yr[it].astype(F32) + beta * yold[...]
         yold[...] = yy
         wy = w_ref[...] * yy
         u = wy.astype(BF16)
@@ -375,7 +375,8 @@
             v((i2, n, cols, width), BF16),
             v((i2, depth + 4, 8, 128), F32),
             v((cols, rows_dev), F32),
-            v((i2, cols, rows_dev), F32),
+            v((cols, rows_dev), BF16),
+            v((i2, cols, rows_dev), BF16),
             v((cols, rows_dev), F32),
             v((i2, 8, 128), F32),
             v((i2, 8, 128), F32),

time: 61.7 us -> 59.5 us (0.964)
  Pallas kernels: 56.5 us -> 54.3 us
    pallas_call x1, Pallas kernels: 56.5 us -> 54.3 us  [fused(): pl.pallas_call(functools.partial(solve_kernel, depth, total_rows), out_sh...]
where the time goes in v3:
time: 59.5 us; the launch traced here: 59.2 us
  Pallas kernels  54.3 us (91%)
  local copies, waits for them, and re-layouts  4.28 us (7%)
  between operations  0.65 us (1%)
    pallas_call x1, Pallas kernels, fused(): pl.pallas_call(functools.partial(solve_kernel, depth, total_rows), out_sh...  54.3 us
    unnamed x10, local copies, waits for them, and re-layouts  4.28 us

profile of v3, /device:TPU:0, one launch (start us, length us, event | category | flops | bytes accessed | tf_op | source)
XLA Modules:
  0.0 59.2 jit_solution(15799830337250919180)
XLA Ops:
  0.6 0.0 copy-start
  0.6 0.8 %copy-done = f32[32,1,512]{2,1,0:T(1,128)S(1)} copy-done((f32[32,1,512]{2,1,0:T(1,128)S(1)}, f32[32,1,512]{2,1,0:T(1,128)}, u32[]{:S(2)}) %copy-start) | copy-done | bytes 65560
  1.5 0.0 copy-start.1
  1.5 0.7 %copy-done.1 = s32[1024]{0:T(1024)S(1)} copy-done((s32[1024]{0:T(1024)S(1)}, s32[1024]{0:T(1024)}, u32[]{:S(2)}) %copy-start.1) | copy-done | bytes 4120
  2.2 0.0 copy-start.2
  2.2 0.7 %copy-done.2 = f32[1024]{0:T(1024)S(1)} copy-done((f32[1024]{0:T(1024)S(1)}, f32[1024]{0:T(1024)}, u32[]{:S(2)}) %copy-start.2) | copy-done | bytes 4120
  2.8 0.0 copy-start.3
  2.8 0.7 %copy-done.3 = f32[1,512]{1,0:T(1,128)S(1)} copy-done((f32[1,512]{1,0:T(1,128)S(1)}, f32[1,512]{1,0:T(1,128)}, u32[]{:S(2)}) %copy-start.3) | copy-done | bytes 2072
  3.5 54.3 %shard_map.68 = (f32[32,512]{1,0:T(8,128)S(1)}, f32[32,512]{1,0:T(8,128)S(1)}) custom-call(bf16[1024,8192]{1,0:T(8,128)(2,1)} %a_hbm.1, s32[1,1024]{1,0:T(1,128)S(1)} %bitcast.6, f32[1,1024]{1,0:T(1,128)S(1)} %bitcast.7, f32[1,512]{1,0:T(1,128)S(1)} %copy-done.3, f32[32,1,512]{2,1,0:T(1,128)S(1)} %copy-done), custom_call_target="tpu_custom_call" | custom-call | tf_op jit(solution)/shard_map/pallas_call | solution.py:363
  57.8 0.7 %copy.7 = f32[32,1,512]{2,1,0:T(1,128)} copy(f32[32,1,512]{2,0,1:T(8,128)S(1)} %bitcast.5) | data formatting | bytes 131072
  58.5 0.7 %copy.8 = f32[32,1,512]{2,1,0:T(1,128)} copy(f32[32,1,512]{2,0,1:T(8,128)S(1)} %bitcast.4) | data formatting | bytes 131072
Async XLA Ops:
  0.6 0.8 %copy-start = (f32[32,1,512]{2,1,0:T(1,128)S(1)}, f32[32,1,512]{2,1,0:T(1,128)}, u32[]{:S(2)}) copy-start(f32[32,1,512]{2,1,0:T(1,128)} %b_in.1) | copy-start | bytes 196612
  1.5 0.7 %copy-start.1 = (s32[1024]{0:T(1024)S(1)}, s32[1024]{0:T(1024)}, u32[]{:S(2)}) copy-start(s32[1024]{0:T(1024)} %param.6) | copy-start | bytes 12292
  2.2 0.7 %copy-start.2 = (f32[1024]{0:T(1024)S(1)}, f32[1024]{0:T(1024)}, u32[]{:S(2)}) copy-start(f32[1024]{0:T(1024)} %param.7) | copy-start | bytes 12292
  2.8 0.7 %copy-start.3 = (f32[1,512]{1,0:T(1,128)S(1)}, f32[1,512]{1,0:T(1,128)}, u32[]{:S(2)}) copy-start(f32[1,512]{1,0:T(1,128)} %d_in.1) | copy-start | bytes 6148
